TPU v7x, 32 devices: a whole 2x2x4 slice. The times are simulated.
32 devices in a mesh: own: 8 (over z, core), help: 4 (over y, x).
Axes of the slice: x: 2, y: 2, z: 4, core: 2. Of those that a mesh axis runs over, the one named last changes fastest.
Arguments:
- records: bfloat16 [16384, 256], P(('own', 'help')), may hold values from -6 to 6
- owner: int32 [16384, 1], P(('own', 'help')), may hold values from 0 to 7; in each aligned block of 512 rows (0 to 511, 512 to 1023, ...) at most 128 rows name the same one
- subkey: int32 [16384], P(('own', 'help')), may hold values from 0 to 3
- source: int32 [16384], P(('own', 'help')), may hold values from 0 to 3
Outputs:
- resolved: bfloat16 [16384, 256], P(('own', 'help'))
Inputs may be any that keep to these rules, and one draw needn't show every extreme that they name: Among the 512 records of one device (aligned blocks of rows), no owner is named more than 128 times, and in every draw some device names some owner exactly 128 times.
All inputs are finite; a program needn't handle non-finite values.
Results may differ from a plain program's by a relative error of at most 0.0052.
Values may be sent and summed in bfloat16 or wider, within the bound.
No kernel may reach another device: no remote copies, remote signals or barrier semaphores. Data moves between devices by JAX's collectives and lax.ppermute only.
A program may use at most 192 MiB of HBM per device.

v0:
```python
import jax
import jax.numpy as jnp
from jax import lax
from jax.sharding import PartitionSpec as P

SOURCES = 4
epsilon = 1e-06
sharpness = 4.0


def normalized(records):
    values_f = records.astype(jnp.float32)
    inverse = lax.rsqrt(jnp.mean(values_f * values_f, axis=1, keepdims=True) + epsilon)
    return (values_f * inverse).astype(jnp.bfloat16)


def pair_weights(query_rows, query_codes, key_rows, key_codes):
    scores = lax.dot_general(
        query_rows, key_rows, (((1,), (1,)), ((), ())), preferred_element_type=jnp.float32
    )
    matched = (query_codes[:, None] >= 0) & (key_codes[None, :] >= 0)
    matched = matched & (query_codes[:, None] // SOURCES == key_codes[None, :] // SOURCES)
    matched = matched & (query_codes[:, None] % SOURCES != key_codes[None, :] % SOURCES)
    return jnp.where(
        matched, jnp.exp(scores * (sharpness / query_rows.shape[1])), jnp.zeros_like(scores)
    )


def resolve(held_rows, partner, mass):
    merged = held_rows.astype(jnp.float32) + partner * lax.rsqrt(1.0 + mass)[:, None]
    return merged.astype(jnp.bfloat16)


def shards(records, owner, subkey, source):
    row_count = records.shape[0]
    width = records.shape[1]
    owners = lax.axis_size("own")
    slot_count = 2 * row_count
    capacity = slot_count // owners
    scaled = normalized(records)
    target = owner[:, 0]
    onehot = (target[:, None] == jnp.arange(owners, dtype=jnp.int32)[None, :]).astype(jnp.int32)
    slot_rank = jnp.sum(jnp.cumsum(onehot, axis=0) * onehot, axis=1) - 1
    slot_index = target * capacity + slot_rank
    outbox = jnp.zeros((slot_count, width), jnp.bfloat16).at[slot_index].set(scaled)
    out_codes = jnp.full((slot_count,), -1, jnp.int32).at[slot_index].set(subkey * SOURCES + source)
    inbox, in_codes = (
        lax.all_to_all(
            outbox.reshape(owners, capacity, width), "own", split_axis=0, concat_axis=0, tiled=True
        ),
        lax.all_to_all(
            out_codes.reshape(owners, capacity), "own", split_axis=0, concat_axis=0, tiled=True
        ),
    )
    held_rows = inbox.reshape(slot_count, width)
    held_codes = in_codes.reshape(slot_count)
    incoming = (
        lax.all_gather(held_rows, "help", axis=0, tiled=True),
        lax.all_gather(held_codes, "help", axis=0, tiled=True),
    )
    weight = pair_weights(held_rows, held_codes, incoming[0], incoming[1])
    partner_next = jnp.dot(
        weight.astype(jnp.bfloat16), incoming[0], preferred_element_type=jnp.float32
    )
    mass = jnp.sum(weight, axis=1)
    merged = resolve(held_rows, partner_next, mass).reshape(owners, capacity, width)
    returned = lax.all_to_all(merged, "own", split_axis=0, concat_axis=0, tiled=True).reshape(
        slot_count, width
    )
    return returned[slot_index]


def solution(mesh):
    return jax.shard_map(
        shards,
        mesh=mesh,
        in_specs=(
            P(("own", "help"), None),
            P(("own", "help"), None),
            P(("own", "help")),
            P(("own", "help")),
        ),
        out_specs=P(("own", "help"), None),
        check_vma=False,
    )
```

profile of v0, /device:TPU:0, one launch (start us, length us, event | category | flops | bytes accessed | tf_op | source)
XLA Modules:
  0.0 117.5 jit_solution(4763169931657767500)
XLA Ops:
  6.5 0.0 all-gather.2.cloned.1.call-start
  6.5 0.7 fusion.20
  7.2 1.1 reduce-window.6
  8.4 0.2 slice_reduce_fusion
  8.6 0.8 fusion.19
  9.4 0.7 compare_select_fusion
  10.1 1.1 fusion.13
  11.2 3.0 %scatter_custom_fusion = bf16[1024,256]{1,0:T(8,128)(2,1)S(1)} fusion(s32[512]{0:T(512)S(1)} %bitcast.30, bf16[512,256]{1,0:T(8,128)(2,1)} %param.4, f32[512]{0:T(512)S(1)} %add_rsqrt_fusion.1, bf16[]{:T(256)} %constant.61.clone.1), kind=kCustom, calls=%fused_computation.14 | custom fusion | flops 393216 | bytes 788482 | tf_op jit(solution)/shard_map/scatter | solution.py:45
  14.2 21.6 %all_to_all.19 = bf16[8,128,256]{2,1,0:T(8,128)(2,1)} all-to-all(bf16[8,128,256]{2,1,0:T(8,128)(2,1)S(1)} %bitcast.23), channel_id=1, replica_groups=mesh['own'=8,'help'=4] {'own'}, dimensions={0} | all-to-all | bytes 1048576 | tf_op jit(solution)/shard_map/all_to_all | solution.py:48
  35.8 0.0 all-gather.2.cloned.1.call-update
  35.8 0.7 multiply_add_fusion
  36.5 2.4 %scatter_custom_fusion.1 = s32[1024]{0:T(1024)S(1)} fusion(s32[512]{0:T(512)S(1)} %bitcast.31, s32[512]{0:T(512)S(1)} %multiply_add_fusion, s32[]{:T(128)} %constant.64.clone.1), kind=kCustom, calls=%fused_computation.45 | custom fusion | bytes 4100 | tf_op jit(solution)/shard_map/scatter | solution.py:46
  38.9 7.9 %all_to_all.20 = s32[8,1,128]{2,1,0:T(1,128)S(1)} all-to-all(s32[8,1,128]{2,1,0:T(1,128)S(1)} %bitcast.29), channel_id=1, replica_groups=mesh['own'=8,'help'=4] {'own'}, dimensions={0} | all-to-all | bytes 8192 | tf_op jit(solution)/shard_map/all_to_all | solution.py:51
  46.9 8.3 %all_gather.6 = s32[4096]{0:T(1024)S(1)} all-gather(s32[1024]{0:T(1024)S(1)} %bitcast.24), channel_id=1, replica_groups=mesh['own'=8,'help'=4] {'help'}, dimensions={0}, use_global_device_ids=true | all-gather | bytes 20480 | tf_op jit(solution)/shard_map/all_gather | solution.py:59
  55.3 15.0 %all-gather.2.cloned.1.call-done = bf16[4096,256]{1,0:T(8,128)(2,1)} async-done(((bf16[1024,256]{1,0:T(8,128)(2,1)}), bf16[4096,256]{1,0:T(8,128)(2,1)}) %all-gather.2.cloned.1.call-update) | async-done | bytes 2097168 | tf_op jit(solution)/shard_map/all_gather | solution.py:58
  70.3 0.0 copy-start
  70.3 0.0 copy-start.1
  70.3 9.7 %fusion = (f32[1024]{0:T(1024)S(1)}, f32[1024,4096]{1,0:T(8,128)S(1)}) fusion(s32[4096]{0:T(1024)S(1)} %get-tuple-element.6, s32[4096]{0:T(1024)S(1)} %get-tuple-element.5, s32[1024]{0:T(1024)S(1)} %get-tuple-element.8, s32[1024]{0:T(1024)S(1)} %get-tuple-element.7, pred[4096]{0:T(1024)(128)(4,1)S(1)} %broadcast_compare_fusion, ...), kind=kOutput, calls=%fused_computation.4 | convolution fusion | flops 2181037056 | bytes 19448832 | tf_op jit(solution)/shard_map/dot_general | solution.py:18
  80.0 0.0 copy-done
  80.0 0.0 copy-done.1
  80.0 8.1 %fusion.10 = bf16[1024,256]{1,0:T(8,128)(2,1)} fusion(bf16[4096,256]{1,0:T(8,128)(2,1)S(1)} %copy-done.1, f32[1024,4096]{1,0:T(8,128)S(1)} %get-tuple-element.10, s32[4096]{0:T(1024)S(1)} %get-tuple-element.6, s32[4096]{0:T(1024)S(1)} %get-tuple-element.5, s32[1024]{0:T(1024)S(1)} %get-tuple-element.8, s32[1024]{0:T(1024)S(1)} %get-tuple-element.7, ...), kind=kOutput, calls=%fused_computation.9 | convolution fusion | flops 2182086656 | bytes 19973120 | tf_op jit(solution)/shard_map/dot_general | solution.py:62
  88.2 4.6 %all-to-all-start.2 = ((bf16[8,128,256]{2,1,0:T(8,128)(2,1)}), bf16[8,128,256]{2,1,0:T(8,128)(2,1)S(1)}, u32[]{:S(2)}, u32[]{:S(2)}) async-start(bf16[8,128,256]{2,1,0:T(8,128)(2,1)} %bitcast.10), calls=%async_computation.2 | async-start | bytes 1048576 | tf_op jit(solution)/shard_map/all_to_all | solution.py:67
  92.8 15.4 %all-to-all-done.2 = bf16[8,128,256]{2,1,0:T(8,128)(2,1)S(1)} async-done(((bf16[8,128,256]{2,1,0:T(8,128)(2,1)}), bf16[8,128,256]{2,1,0:T(8,128)(2,1)S(1)}, u32[]{:S(2)}, u32[]{:S(2)}) %all-to-all-start.2) | async-done | bytes 524320 | tf_op jit(solution)/shard_map/all_to_all | solution.py:67
  108.1 2.6 %gather_fusion = bf16[512,256]{1,0:T(8,128)(2,1)} fusion(bf16[1024,256]{1,0:T(8,128)(2,1)S(1)} %bitcast.19, s32[1024]{0:T(1024)S(1)} %pad_clamp_fusion), kind=kCustom, calls=%fused_computation | custom fusion | bytes 526336 | tf_op jit(solution)/shard_map/gather | solution.py:70
  (10 shorter events, 0.1 us)
Async XLA Ops:
  6.5 63.7 %all-gather.2.cloned.1.call-start = ((), (), s32[]{:S(2)}) async-start(), calls=%async_computation.3 | async-start | bytes 2621440 | tf_op jit(solution)/shard_map/all_gather | solution.py:58
  70.3 9.7 %copy-start = (bf16[8,128,256]{2,1,0:T(8,128)(2,1)S(1)}, bf16[8,128,256]{2,1,0:T(8,128)(2,1)}, u32[]{:S(2)}) copy-start(bf16[8,128,256]{2,1,0:T(8,128)(2,1)} %all_to_all.19) | copy-start | bytes 1572868
  70.3 9.7 %copy-start.1 = (bf16[4096,256]{1,0:T(8,128)(2,1)S(1)}, bf16[4096,256]{1,0:T(8,128)(2,1)}, u32[]{:S(2)}) copy-start(bf16[4096,256]{1,0:T(8,128)(2,1)} %all-gather.2.cloned.1.call-done) | copy-start | bytes 6291460
  88.2 20.0 %all-to-all-start.2 = ((bf16[8,128,256]{2,1,0:T(8,128)(2,1)}), bf16[8,128,256]{2,1,0:T(8,128)(2,1)S(1)}, u32[]{:S(2)}, u32[]{:S(2)}) async-start(bf16[8,128,256]{2,1,0:T(8,128)(2,1)} %bitcast.10), calls=%async_computation.2 | async-start | bytes 1048576 | tf_op jit(solution)/shard_map/all_to_all | solution.py:67
Sparse Core Ops, SparseCore 0:
  35.9 34.2 all-gather.1
where the time goes:
time: 118 us
  blocking collectives  37.8 us (32%)
  waiting for transfers between devices  30.4 us (26%)
  matrix products  17.9 us (15%)
  between operations  13.5 us (11%)
  other arithmetic  8.15 us (7%)
  local copies, waits for them, and re-layouts  5.24 us (4%)
  starting transfers between devices  4.61 us (4%)
    all_to_all x1, blocking collectives, shards(): lax.all_to_all(outbox.reshape(owners, capacity, width), 'own', split_axis...  21.6 us
    all_to_all x1, waiting for transfers between devices, shards(): lax.all_to_all(merged, 'own', split_axis=0, concat_axis=0, tiled=True)  15.4 us
    all_gather x1, waiting for transfers between devices, shards(): lax.all_gather(held_rows, 'help', axis=0, tiled=True)  15 us
    dot_general x1, matrix products, pair_weights(): lax.dot_general(query_rows, key_rows, (((1,), (1,)), ((), ())), preferred...  9.72 us
    all_gather x1, blocking collectives, shards(): lax.all_gather(held_codes, 'help', axis=0, tiled=True)  8.34 us
    dot_general x1, matrix products, shards(): jnp.dot(weight.astype(jnp.bfloat16), incoming[0], preferred_element_type=...  8.14 us
    all_to_all x1, blocking collectives, shards(): lax.all_to_all(out_codes.reshape(owners, capacity), 'own', split_axis=0,...  7.92 us
    all_to_all x1, starting transfers between devices, shards(): lax.all_to_all(merged, 'own', split_axis=0, concat_axis=0, tiled=True)  4.61 us
  transfers between devices with their start and end apart: 2, of which 2 were waited for; matrix products, arithmetic and copies ran while one was open for 3% of the time, Pallas kernels for 0%

commit v1 on v0

--- a/solution.py
+++ b/solution.py
@@ -6,6 +6,29 @@
 SOURCES = 4
 epsilon = 1e-06
 sharpness = 4.0
+
+
+def split_up(value, dim, size):
+    lengths = value.shape
+    blocks = value.reshape(*lengths[:dim], size, lengths[dim] // size, *lengths[dim + 1 :])
+    return jnp.moveaxis(blocks, dim, 0)
+
+
+def laid_out(blocks, dim):
+    shape = list(blocks.shape[1:])
+    shape[dim] *= blocks.shape[0]
+    return jnp.moveaxis(blocks, 0, dim).reshape(shape)
+
+
+def exchange_in_pairs(array, axis, split_dim, concat_dim):
+    count, index = (lax.axis_size(axis), lax.axis_index(axis))
+    pieces = split_up(array, split_dim, count)
+    gathered = [pieces[index]]
+    for step in range(1, count):
+        sent = pieces[index ^ step]
+        gathered.append(lax.ppermute(sent, axis, [(i, i ^ step) for i in range(count)]))
+    pieces = jnp.stack(gathered)[index ^ jnp.arange(count)]
+    return laid_out(pieces, concat_dim)
 
 
 def normalized(records):
@@ -64,9 +87,7 @@
     )
     mass = jnp.sum(weight, axis=1)
     merged = resolve(held_rows, partner_next, mass).reshape(owners, capacity, width)
-    returned = lax.all_to_all(merged, "own", split_axis=0, concat_axis=0, tiled=True).reshape(
-        slot_count, width
-    )
+    returned = exchange_in_pairs(merged, "own", 0, 0).reshape(slot_count, width)
     return returned[slot_index]
 
 

time: 118 us -> 113 us (0.958)
  blocking collectives: 37.8 us -> 29.9 us
  starting transfers between devices: 4.61 us -> 11.5 us
  waiting for transfers between devices: 30.4 us -> 25.6 us
  local copies, waits for them, and re-layouts: 5.24 us -> 6.49 us
    all_to_all x1, waiting for transfers between devices: 15.4 us -> 5.34 us  [shards(): lax.all_to_all(out_codes.reshape(owners, capacity), 'own', split_axis=0,...]
    ppermute x0 -> x7, starting transfers between devices: none -> 8.18 us  [exchange_in_pairs(): lax.ppermute(sent, axis, [(i, i ^ step) for i in range(count)])]
    all_to_all x1 -> x0, blocking collectives: 7.92 us -> none  [shards(): lax.all_to_all(out_codes.reshape(owners, capacity), 'own', split_axis=0,...]
    ppermute x0 -> x7, waiting for transfers between devices: none -> 6.62 us  [exchange_in_pairs(): lax.ppermute(sent, axis, [(i, i ^ step) for i in range(count)])]
    all_gather x1, waiting for transfers between devices: 15 us -> 13.6 us  [shards(): lax.all_gather(held_rows, 'help', axis=0, tiled=True)]
    all_to_all x1, starting transfers between devices: 4.61 us -> 3.31 us  [shards(): lax.all_to_all(out_codes.reshape(owners, capacity), 'own', split_axis=0,...]
  transfers between devices with their start and end apart: 2 -> 9, of which waited for: 2 -> 3; matrix products, arithmetic and copies ran while one was open for 3% -> 3% of each run, Pallas kernels for 0% -> 0%
where the time goes in v1:
time: 113 us; the launch traced here: 112 us
  blocking collectives  29.9 us (26%)
  waiting for transfers between devices  25.6 us (23%)
  matrix products  17 us (15%)
  between operations  13.6 us (12%)
  starting transfers between devices  11.5 us (10%)
  other arithmetic  8.17 us (7%)
  local copies, waits for them, and re-layouts  6.49 us (6%)
    all_to_all x1, blocking collectives, shards(): lax.all_to_all(outbox.reshape(owners, capacity, width), 'own', split_axis...  21.6 us
    all_gather x1, waiting for transfers between devices, shards(): lax.all_gather(held_rows, 'help', axis=0, tiled=True)  13.6 us
    dot_general x1, matrix products, pair_weights(): lax.dot_general(query_rows, key_rows, (((1,), (1,)), ((), ())), preferred...  9.72 us
    all_gather x1, blocking collectives, shards(): lax.all_gather(held_codes, 'help', axis=0, tiled=True)  8.34 us
    ppermute x7, starting transfers between devices, exchange_in_pairs(): lax.ppermute(sent, axis, [(i, i ^ step) for i in range(count)])  8.18 us
    dot_general x1, matrix products, shards(): jnp.dot(weight.astype(jnp.bfloat16), incoming[0], preferred_element_type=...  7.27 us
    ppermute x7, waiting for transfers between devices, exchange_in_pairs(): lax.ppermute(sent, axis, [(i, i ^ step) for i in range(count)])  6.62 us
    all_to_all x1, waiting for transfers between devices, shards(): lax.all_to_all(out_codes.reshape(owners, capacity), 'own', split_axis=0,...  5.34 us
  transfers between devices with their start and end apart: 9, of which 3 were waited for; matrix products, arithmetic and copies ran while one was open for 3% of the time, Pallas kernels for 0%

profile of v1, /device:TPU:0, one launch (start us, length us, event | category | flops | bytes accessed | tf_op | source)
XLA Modules:
  0.0 112.3 jit_solution(1630167143927092335)
XLA Ops:
  6.5 0.0 all-gather.2.cloned.1.call-start
  6.5 0.7 fusion.20
  7.2 1.1 %reduce-window.6 = s32[8,4,128]{2,0,1:T(8,128)S(1)} reduce-window(s32[8,4,128]{2,0,1:T(8,128)S(1)} %fusion.20, s32[]{:T(128)} %constant.45.clone.1), window={size=1x1x128 pad=0_0x0_0x127_0}, to_apply=%region_0.0 | reduce-window | flops 520192 | bytes 32772 | tf_op jit(solution)/shard_map/reduce-window
  8.4 0.2 slice_reduce_fusion
  8.6 0.8 fusion.19
  9.4 0.7 compare_select_fusion
  10.1 1.1 fusion.13
  11.2 3.0 %scatter_custom_fusion = bf16[1024,256]{1,0:T(8,128)(2,1)S(1)} fusion(s32[512]{0:T(512)S(1)} %bitcast.62, bf16[512,256]{1,0:T(8,128)(2,1)} %param.4, f32[512]{0:T(512)S(1)} %add_rsqrt_fusion.1, bf16[]{:T(256)} %constant.40.clone.1), kind=kCustom, calls=%fused_computation.15 | custom fusion | flops 393216 | bytes 788482 | tf_op jit(solution)/shard_map/scatter | solution.py:68
  14.2 21.6 %all_to_all.14 = bf16[8,128,256]{2,1,0:T(8,128)(2,1)} all-to-all(bf16[8,128,256]{2,1,0:T(8,128)(2,1)S(1)} %bitcast.54), channel_id=1, replica_groups=mesh['own'=8,'help'=4] {'own'}, dimensions={0} | all-to-all | bytes 1048576 | tf_op jit(solution)/shard_map/all_to_all | solution.py:71
  35.8 0.0 all-gather.2.cloned.1.call-update
  35.8 0.7 multiply_add_fusion
  36.5 3.0 %scatter_custom_fusion.1 = s32[1024]{0:T(1024)} fusion(s32[512]{0:T(512)S(1)} %bitcast.63, s32[512]{0:T(512)S(1)} %multiply_add_fusion, s32[]{:T(128)} %constant.46.clone.1), kind=kCustom, calls=%fused_computation.63 | custom fusion | bytes 4100 | tf_op jit(solution)/shard_map/scatter | solution.py:69
  39.5 3.3 %all-to-all-start.1 = ((s32[8,1,128]{2,1,0:T(1,128)}), s32[8,1,128]{2,1,0:T(1,128)S(1)}, u32[]{:S(2)}, u32[]{:S(2)}) async-start(s32[8,1,128]{2,1,0:T(1,128)} %bitcast.8), calls=%async_computation.1 | async-start | bytes 8192 | tf_op jit(solution)/shard_map/all_to_all | solution.py:74
  42.9 5.3 %all-to-all-done.1 = s32[8,1,128]{2,1,0:T(1,128)S(1)} async-done(((s32[8,1,128]{2,1,0:T(1,128)}), s32[8,1,128]{2,1,0:T(1,128)S(1)}, u32[]{:S(2)}, u32[]{:S(2)}) %all-to-all-start.1) | async-done | bytes 4128 | tf_op jit(solution)/shard_map/all_to_all | solution.py:74
  48.2 8.3 %all_gather.6 = s32[4096]{0:T(1024)S(1)} all-gather(s32[1024]{0:T(1024)S(1)} %bitcast.57), channel_id=1, replica_groups=mesh['own'=8,'help'=4] {'help'}, dimensions={0}, use_global_device_ids=true | all-gather | bytes 20480 | tf_op jit(solution)/shard_map/all_gather | solution.py:82
  56.6 13.6 %all-gather.2.cloned.1.call-done = bf16[4096,256]{1,0:T(8,128)(2,1)} async-done(((bf16[1024,256]{1,0:T(8,128)(2,1)}), bf16[4096,256]{1,0:T(8,128)(2,1)}) %all-gather.2.cloned.1.call-update) | async-done | bytes 2097168 | tf_op jit(solution)/shard_map/all_gather | solution.py:81
  70.3 0.0 copy-start
  70.3 0.0 copy-start.1
  70.3 9.7 %fusion = (f32[1024]{0:T(1024)S(1)}, f32[1024,4096]{1,0:T(8,128)S(1)}) fusion(s32[4096]{0:T(1024)S(1)} %get-tuple-element.14, s32[4096]{0:T(1024)S(1)} %get-tuple-element.13, s32[1024]{0:T(1024)S(1)} %get-tuple-element.16, s32[1024]{0:T(1024)S(1)} %get-tuple-element.15, pred[4096]{0:T(1024)(128)(4,1)S(1)} %broadcast_compare_fusion, ...), kind=kOutput, calls=%fused_computation.5 | convolution fusion | flops 2181037056 | bytes 19448832 | tf_op jit(solution)/shard_map/dot_general | solution.py:41
  80.0 0.0 copy-done
  80.0 0.0 copy-done.1
  80.0 7.3 %fusion.10 = bf16[1024,256]{1,0:T(8,128)(2,1)S(1)} fusion(bf16[4096,256]{1,0:T(8,128)(2,1)S(1)} %copy-done.1, f32[1024,4096]{1,0:T(8,128)S(1)} %get-tuple-element.18, s32[4096]{0:T(1024)S(1)} %get-tuple-element.14, s32[4096]{0:T(1024)S(1)} %get-tuple-element.13, s32[1024]{0:T(1024)S(1)} %get-tuple-element.16, s32[1024]{0:T(1024)S(1)} %get-tuple-element.15, ...), kind=kOutput, calls=%fused_computation.10 | convolution fusion | flops 2182086656 | bytes 19973120 | tf_op jit(solution)/shard_map/dot_general | solution.py:85
  87.3 0.1 dynamic-slice_bitcast_fusion
  87.4 0.1 collective-permute-start
  87.5 1.6 %collective-permute-start.1 = (bf16[1,128,256]{2,1,0:T(8,128)(2,1)S(1)}, bf16[1,128,256]{2,1,0:T(8,128)(2,1)S(1)}, u32[]{:S(2)}, u32[]{:S(2)}) collective-permute-start(bf16[1,128,256]{2,1,0:T(8,128)(2,1)S(1)} %get-tuple-element.10), channel_id=1, source_target_pairs={{0,8},{4,12},{8,0},{12,4},{16,24},{20,28},{24,16},{28,20},{1,9},{5... | collective-permute-start | bytes 196616 | tf_op jit(solution)/shard_map/ppermute | solution.py:29
  89.0 0.3 collective-permute-start.2
  89.3 2.4 %collective-permute-start.3 = (bf16[1,128,256]{2,1,0:T(8,128)(2,1)S(1)}, bf16[1,128,256]{2,1,0:T(8,128)(2,1)S(1)}, u32[]{:S(2)}, u32[]{:S(2)}) collective-permute-start(bf16[1,128,256]{2,1,0:T(8,128)(2,1)S(1)} %get-tuple-element.8), channel_id=1, source_target_pairs={{0,16},{4,20},{8,24},{12,28},{16,0},{20,4},{24,8},{28,12},{1,17},{... | collective-permute-start | bytes 196616 | tf_op jit(solution)/shard_map/ppermute | solution.py:29
  91.7 0.2 collective-permute-start.4
  91.9 0.0 collective-permute-done
  91.9 3.3 %collective-permute-start.5 = (bf16[1,128,256]{2,1,0:T(8,128)(2,1)S(1)}, bf16[1,128,256]{2,1,0:T(8,128)(2,1)S(1)}, u32[]{:S(2)}, u32[]{:S(2)}) collective-permute-start(bf16[1,128,256]{2,1,0:T(8,128)(2,1)S(1)} %get-tuple-element.6), channel_id=1, source_target_pairs={{0,24},{4,28},{8,16},{12,20},{16,8},{20,12},{24,0},{28,4},{1,25},{... | collective-permute-start | bytes 196616 | tf_op jit(solution)/shard_map/ppermute | solution.py:29
  95.2 0.0 collective-permute-done.1
  95.3 0.3 collective-permute-start.6
  95.6 0.0 collective-permute-done.2
  95.6 0.0 collective-permute-done.3
  95.6 6.6 %collective-permute-done.4 = bf16[1,128,256]{2,1,0:T(8,128)(2,1)S(1)} collective-permute-done((bf16[1,128,256]{2,1,0:T(8,128)(2,1)S(1)}, bf16[1,128,256]{2,1,0:T(8,128)(2,1)S(1)}, u32[]{:S(2)}, u32[]{:S(2)}) %collective-permute-start.4) | collective-permute-done | bytes 65568 | tf_op jit(solution)/shard_map/ppermute | solution.py:29
  102.2 0.0 collective-permute-done.5
  102.3 0.0 collective-permute-done.6
  102.3 0.6 gather_fusion
  102.9 2.6 %gather_fusion.1 = bf16[512,256]{1,0:T(8,128)(2,1)} fusion(bf16[1024,256]{1,0:T(8,128)(2,1)S(1)} %bitcast.50, s32[1024]{0:T(1024)S(1)} %pad_clamp_fusion), kind=kCustom, calls=%fused_computation.1 | custom fusion | bytes 526336 | tf_op jit(solution)/shard_map/gather | solution.py:91
  (19 shorter events, 0.2 us)
Async XLA Ops:
  6.5 63.7 %all-gather.2.cloned.1.call-start = ((), (), s32[]{:S(2)}) async-start(), calls=%async_computation.2 | async-start | bytes 2621440 | tf_op jit(solution)/shard_map/all_gather | solution.py:81
  39.5 8.7 %all-to-all-start.1 = ((s32[8,1,128]{2,1,0:T(1,128)}), s32[8,1,128]{2,1,0:T(1,128)S(1)}, u32[]{:S(2)}, u32[]{:S(2)}) async-start(s32[8,1,128]{2,1,0:T(1,128)} %bitcast.8), calls=%async_computation.1 | async-start | bytes 8192 | tf_op jit(solution)/shard_map/all_to_all | solution.py:74
  70.3 9.7 %copy-start = (bf16[8,128,256]{2,1,0:T(8,128)(2,1)S(1)}, bf16[8,128,256]{2,1,0:T(8,128)(2,1)}, u32[]{:S(2)}) copy-start(bf16[8,128,256]{2,1,0:T(8,128)(2,1)} %all_to_all.14) | copy-start | bytes 1572868
  70.3 9.7 %copy-start.1 = (bf16[4096,256]{1,0:T(8,128)(2,1)S(1)}, bf16[4096,256]{1,0:T(8,128)(2,1)}, u32[]{:S(2)}) copy-start(bf16[4096,256]{1,0:T(8,128)(2,1)} %all-gather.2.cloned.1.call-done) | copy-start | bytes 6291460
  87.4 4.6 %collective-permute-start = (bf16[1,128,256]{2,1,0:T(8,128)(2,1)S(1)}, bf16[1,128,256]{2,1,0:T(8,128)(2,1)S(1)}, u32[]{:S(2)}, u32[]{:S(2)}) collective-permute-start(bf16[1,128,256]{2,1,0:T(8,128)(2,1)S(1)} %get-tuple-element.11), channel_id=1, source_target_pairs={{0,4},{4,0},{8,12},{12,8},{16,20},{20,16},{24,28},{28,24},{1,5},{5... | collective-permute-start | bytes 196616 | tf_op jit(solution)/shard_map/ppermute | solution.py:29
  87.5 7.8 %collective-permute-start.1 = (bf16[1,128,256]{2,1,0:T(8,128)(2,1)S(1)}, bf16[1,128,256]{2,1,0:T(8,128)(2,1)S(1)}, u32[]{:S(2)}, u32[]{:S(2)}) collective-permute-start(bf16[1,128,256]{2,1,0:T(8,128)(2,1)S(1)} %get-tuple-element.10), channel_id=1, source_target_pairs={{0,8},{4,12},{8,0},{12,4},{16,24},{20,28},{24,16},{28,20},{1,9},{5... | collective-permute-start | bytes 196616 | tf_op jit(solution)/shard_map/ppermute | solution.py:29
  89.0 6.6 %collective-permute-start.2 = (bf16[1,128,256]{2,1,0:T(8,128)(2,1)S(1)}, bf16[1,128,256]{2,1,0:T(8,128)(2,1)S(1)}, u32[]{:S(2)}, u32[]{:S(2)}) collective-permute-start(bf16[1,128,256]{2,1,0:T(8,128)(2,1)S(1)} %get-tuple-element.9), channel_id=1, source_target_pairs={{0,12},{4,8},{8,4},{12,0},{16,28},{20,24},{24,20},{28,16},{1,13},{... | collective-permute-start | bytes 196616 | tf_op jit(solution)/shard_map/ppermute | solution.py:29
  89.3 6.3 %collective-permute-start.3 = (bf16[1,128,256]{2,1,0:T(8,128)(2,1)S(1)}, bf16[1,128,256]{2,1,0:T(8,128)(2,1)S(1)}, u32[]{:S(2)}, u32[]{:S(2)}) collective-permute-start(bf16[1,128,256]{2,1,0:T(8,128)(2,1)S(1)} %get-tuple-element.8), channel_id=1, source_target_pairs={{0,16},{4,20},{8,24},{12,28},{16,0},{20,4},{24,8},{28,12},{1,17},{... | collective-permute-start | bytes 196616 | tf_op jit(solution)/shard_map/ppermute | solution.py:29
  91.7 10.5 %collective-permute-start.4 = (bf16[1,128,256]{2,1,0:T(8,128)(2,1)S(1)}, bf16[1,128,256]{2,1,0:T(8,128)(2,1)S(1)}, u32[]{:S(2)}, u32[]{:S(2)}) collective-permute-start(bf16[1,128,256]{2,1,0:T(8,128)(2,1)S(1)} %get-tuple-element.7), channel_id=1, source_target_pairs={{0,20},{4,16},{8,28},{12,24},{16,4},{20,0},{24,12},{28,8},{1,21},{... | collective-permute-start | bytes 196616 | tf_op jit(solution)/shard_map/ppermute | solution.py:29
  91.9 10.3 %collective-permute-start.5 = (bf16[1,128,256]{2,1,0:T(8,128)(2,1)S(1)}, bf16[1,128,256]{2,1,0:T(8,128)(2,1)S(1)}, u32[]{:S(2)}, u32[]{:S(2)}) collective-permute-start(bf16[1,128,256]{2,1,0:T(8,128)(2,1)S(1)} %get-tuple-element.6), channel_id=1, source_target_pairs={{0,24},{4,28},{8,16},{12,20},{16,8},{20,12},{24,0},{28,4},{1,25},{... | collective-permute-start | bytes 196616 | tf_op jit(solution)/shard_map/ppermute | solution.py:29
  95.3 7.0 %collective-permute-start.6 = (bf16[1,128,256]{2,1,0:T(8,128)(2,1)S(1)}, bf16[1,128,256]{2,1,0:T(8,128)(2,1)S(1)}, u32[]{:S(2)}, u32[]{:S(2)}) collective-permute-start(bf16[1,128,256]{2,1,0:T(8,128)(2,1)S(1)} %get-tuple-element.5), channel_id=1, source_target_pairs={{0,28},{4,24},{8,20},{12,16},{16,12},{20,8},{24,4},{28,0},{1,29},{... | collective-permute-start | bytes 196616 | tf_op jit(solution)/shard_map/ppermute | solution.py:29
Sparse Core Ops, SparseCore 0:
  35.9 34.2 all-gather.1
